TPU v7x, 32 devices: a whole 2x2x4 slice. The times are simulated.
32 devices in a mesh: grp: 2 (over y), row: 8 (over z, x), col: 2 (over core).
Axes of the slice: x: 2, y: 2, z: 4, core: 2. Of those that a mesh axis runs over, the one named last changes fastest.
Arguments:
- grad_out: bfloat16 [1024, 8192], P(('grp', 'row'), 'col'), parts along dimension 0, may hold values from -6 to 6
- hidden_act: bfloat16 [1024, 22016], P(('grp', 'col'), 'row'), parts along dimension 0, may hold values from -6 to 6
- down_weight: bfloat16 [22016, 8192], P('row', 'col'), may hold values from -0.0390625 to 0.0390625
- proj_in: bfloat16 [22016, 64], P('row'), may hold values from -0.0390625 to 0.0390625
- proj_out: bfloat16 [8192, 64], P('col'), may hold values from -0.0625 to 0.0625
- queries: bfloat16 [128, 4096], P('row', 'col'), may hold values from -0.01171875 to 0.01171875
- example_ids: int32 [1024], P(('grp', 'row')), parts along dimension 0, may hold values from 0 to 7, never falling along the last dimension, each value on 1 to 128 neighbouring positions
Outputs:
- grad_hidden: bfloat16 [1024, 22016], P(('grp', 'col'), 'row'), parts along dimension 0
- weight_grad: bfloat16 [44032, 8192], P(('grp', 'row'), 'col'), parts along dimension 0
- scores: float32 [128, 16], P(('row', 'col'), 'grp'), parts along dimension 1
There are 2 independent parts, one for each index of `grp`. A program takes and returns all parts, laid end to end along the dimension named above; an argument that names none is the same for every part. Nothing has to cross between parts.
Inputs may be any that keep to these rules, and one draw needn't show every extreme that they name: `example_ids`: never falling along the tokens; each example holds 1 to 128 tokens, one exactly 128.
All inputs are finite; a program needn't handle non-finite values.
Results may differ from a plain program's by a relative error of at most 0.001.
Values may be sent and summed in bfloat16 or wider, within the bound.
A program may use at most 192 MiB of HBM per device.

v0:
```python
import jax
import jax.numpy as jnp
from jax import lax
from jax.sharding import PartitionSpec as P

EXAMPLES = 8


def body(grad_out, hidden_act, down_weight, proj_in, proj_out, queries, example_ids):
    full_hidden = lax.all_gather(hidden_act, "col", axis=0, tiled=True)
    full_grad = lax.all_gather(grad_out, "row", axis=0, tiled=True)
    token_rows = full_grad
    grad_hidden = lax.psum_scatter(
        lax.dot_general(
            token_rows, down_weight, (((1,), (1,)), ((), ())), preferred_element_type=jnp.float32
        ),
        "col",
        scatter_dimension=0,
        tiled=True,
    ).astype(jnp.bfloat16)
    weight_grad = lax.dot_general(
        full_hidden, full_grad, (((0,), (0,)), ((), ())), preferred_element_type=jnp.float32
    ).astype(jnp.bfloat16)
    token_rows = full_hidden
    in_factor = lax.psum_scatter(
        jnp.dot(token_rows, proj_in, preferred_element_type=jnp.float32),
        "row",
        scatter_dimension=0,
        tiled=True,
    )
    out_factor = lax.psum(jnp.dot(grad_out, proj_out, preferred_element_type=jnp.float32), "col")
    split_rank = in_factor.shape[1] // lax.axis_size("col")
    own_factor = lax.dynamic_slice_in_dim(
        in_factor, lax.axis_index("col") * split_rank, split_rank, 1
    )
    outer_terms = (own_factor[:, :, None] * out_factor[:, None, :]).reshape(own_factor.shape[0], -1)
    labels = jnp.arange(EXAMPLES, dtype=jnp.int32)
    onehot = (example_ids[None, :] == labels[:, None]).astype(jnp.float32)
    partial_grads = jnp.dot(onehot, outer_terms, precision=lax.Precision.HIGHEST)
    example_grads = lax.psum(partial_grads, "row")
    values = jnp.dot(queries.astype(jnp.float32), example_grads.T, precision=lax.Precision.HIGHEST)
    scores = lax.psum_scatter(values, "col", scatter_dimension=0, tiled=True)
    return (grad_hidden, weight_grad, scores)


def solution(mesh):
    return jax.shard_map(
        body,
        mesh=mesh,
        in_specs=(
            P(("grp", "row"), "col"),
            P(("grp", "col"), "row"),
            P("row", "col"),
            P("row", None),
            P("col", None),
            P("row", "col"),
            P(("grp", "row")),
        ),
        out_specs=(P(("grp", "col"), "row"), P(("grp", "row"), "col"), P(("row", "col"), "grp")),
        check_vma=False,
    )
```

profile of v0, /device:TPU:0, one launch (start us, length us, event | category | flops | bytes accessed | tf_op | source)
XLA Modules:
  0.0 267.6 jit_solution(11298728215527538428)
XLA Ops:
  7.2 0.0 copy-start
  7.2 0.0 copy-start.1
  7.2 0.0 all-gather.5.cloned.1.call-start
  7.2 0.7 all-gather.5.cloned.1.call-update
  7.9 0.0 copy-start.3
  7.9 0.0 reduce-scatter.6.cloned.1.call-start
  8.0 15.3 %all-gather.5.cloned.1.call-done = bf16[512,2752]{0,1:T(8,128)(2,1)} async-done(((bf16[256,2752]{0,1:T(8,128)(2,1)}), bf16[512,2752]{0,1:T(8,128)(2,1)}) %all-gather.5.cloned.1.call-update) | async-done | bytes 2818064 | tf_op jit(solution)/shard_map/all_gather | solution.py:10
  23.3 3.5 %fusion.3 = f32[512,64]{1,0:T(8,128)} fusion(bf16[512,2752]{0,1:T(8,128)(2,1)} %all-gather.5.cloned.1.call-done, bf16[2752,64]{0,1:T(8,128)(2,1)} %param.10), kind=kOutput, calls=%fused_computation.9 | convolution fusion | flops 180355072 | bytes 3301376 | tf_op jit(solution)/shard_map/dot_general | solution.py:26
  26.8 0.0 reduce-scatter.6.cloned.1.call-update
  26.8 0.0 all-gather.3.cloned.1.call-start
  26.9 0.7 all-gather.3.cloned.1.call-update
  27.6 0.0 all-reduce.3.cloned.1.call-start
  27.6 0.0 copy-done
  27.6 0.0 copy-done.1
  27.6 0.3 fusion.4
  27.9 3.5 %psum.14 = f32[64,64]{1,0:T(8,128)S(1)} all-reduce(f32[64,64]{1,0:T(8,128)S(1)} %fusion.4), channel_id=1, replica_groups=mesh['grp'=2,'row'=8,'col'=2] {'col'}, use_global_device_ids=true, to_apply=%region_2.0 | all-reduce | flops 4096 | bytes 32768 | tf_op jit(solution)/shard_map/psum | solution.py:31
  31.4 59.1 %reduce-scatter.6.cloned.1.call-done = f32[64,64]{1,0:T(8,128)} async-done(((f32[512,64]{1,0:T(8,128)}), f32[64,64]{1,0:T(8,128)}) %reduce-scatter.6.cloned.1.call-update) | async-done | bytes 16400 | tf_op jit(solution)/shard_map/reduce_scatter | solution.py:25
  90.5 0.8 constant_dynamic-slice_fusion.1
  91.3 0.3 broadcast_multiply_fusion
  91.7 0.4 mul.24
  92.1 0.0 copy-done.3
  92.1 0.9 fusion
  93.0 0.0 all-reduce.3.cloned.1.call-update
  93.0 0.0 reduce-scatter.4.cloned.1.call-start
  93.1 71.5 %all-gather.3.cloned.1.call-done = bf16[512,4096]{1,0:T(8,128)(2,1)} async-done(((bf16[64,4096]{1,0:T(8,128)(2,1)}), bf16[512,4096]{1,0:T(8,128)(2,1)}) %all-gather.3.cloned.1.call-update) | async-done | bytes 4194320 | tf_op jit(solution)/shard_map/all_gather | solution.py:11
  164.5 19.1 %fusion.2 = f32[512,2752]{0,1:T(8,128)} fusion(bf16[512,4096]{1,0:T(8,128)(2,1)} %all-gather.3.cloned.1.call-done, bf16[2752,4096]{1,0:T(8,128)(2,1)} %param.9), kind=kOutput, calls=%fused_computation.8 | convolution fusion | flops 11542724608 | bytes 32374784 | tf_op jit(solution)/shard_map/dot_general | solution.py:14
  183.6 0.0 copy-start.5
  183.6 0.0 copy-start.2
  183.6 0.0 copy-start.4
  183.6 0.0 reduce-scatter.4.cloned.1.call-update
  183.7 0.6 copy-done.5
  184.3 0.6 dynamic-slice
  185.5 50.7 %all-reduce.3.cloned.1.call-done = f32[8,2048]{1,0:T(8,128)} async-done(((f32[8,2048]{1,0:T(8,128)}), f32[8,2048]{1,0:T(8,128)}) %all-reduce.3.cloned.1.call-update) | async-done | bytes 65552 | tf_op jit(solution)/shard_map/psum | solution.py:40
  236.2 0.0 copy-done.2
  236.2 1.0 convolution_bitcast_fusion
  237.2 2.5 all-reduce
  239.7 0.1 constant_dynamic-slice_fusion
  239.8 0.7 copy.11
  240.5 0.0 copy-done.4
  240.5 17.6 %convolution_convert_fusion = bf16[2752,4096]{1,0:T(8,128)(2,1)} fusion(bf16[512,2752]{0,1:T(8,128)(2,1)S(1)} %copy-done.4, bf16[512,4096]{1,0:T(8,128)(2,1)} %all-gather.3.cloned.1.call-done), kind=kOutput, calls=%fused_computation | convolution fusion | flops 11553996800 | bytes 29556736 | tf_op jit(solution)/shard_map/dot_general | solution.py:21
  258.0 0.0 reduce-scatter.4.cloned.1.call-done
  258.0 3.0 %convert_element_type.8 = bf16[256,2752]{0,1:T(8,128)(2,1)} convert(f32[256,2752]{0,1:T(8,128)} %reduce-scatter.4.cloned.1.call-done) | non-fusion elementwise | flops 704512 | bytes 4227072 | tf_op jit(solution)/shard_map/convert_element_type | solution.py:20
Async XLA Ops:
  7.2 20.5 %copy-start = (bf16[4096,64]{0,1:T(8,128)(2,1)S(1)}, bf16[4096,64]{0,1:T(8,128)(2,1)}, u32[]{:S(2)}) copy-start(bf16[4096,64]{0,1:T(8,128)(2,1)} %param.11) | copy-start | bytes 1572868
  7.2 20.4 %copy-start.1 = (bf16[64,4096]{1,0:T(8,128)(2,1)S(1)}, bf16[64,4096]{1,0:T(8,128)(2,1)}, u32[]{:S(2)}) copy-start(bf16[64,4096]{1,0:T(8,128)(2,1)} %param.7) | copy-start | bytes 1572868
  7.2 16.1 %all-gather.5.cloned.1.call-start = ((), (), s32[]{:S(2)}) async-start(), calls=%async_computation.4 | async-start | bytes 4227072 | tf_op jit(solution)/shard_map/all_gather | solution.py:10
  7.9 84.1 %copy-start.3 = (s32[64]{0:T(128)S(1)}, s32[64]{0:T(128)}, u32[]{:S(2)}) copy-start(s32[64]{0:T(128)} %param.13) | copy-start | bytes 772
  7.9 82.6 %reduce-scatter.6.cloned.1.call-start = ((), (), s32[]{:S(2)}) async-start(), calls=%async_computation.5 | async-start | bytes 294912 | tf_op jit(solution)/shard_map/reduce_scatter | solution.py:25
  26.8 137.7 %all-gather.3.cloned.1.call-start = ((), (), s32[]{:S(2)}) async-start(), calls=%async_computation.2 | async-start | bytes 4718592 | tf_op jit(solution)/shard_map/all_gather | solution.py:11
  27.6 208.7 %all-reduce.3.cloned.1.call-start = ((), (), s32[]{:S(2)}) async-start(), calls=%async_computation.6 | async-start | bytes 131072 | tf_op jit(solution)/shard_map/psum | solution.py:40
  93.0 165.0 %reduce-scatter.4.cloned.1.call-start = ((), (), s32[]{:S(2)}) async-start(), calls=%async_computation.3 | async-start | bytes 8454144 | tf_op jit(solution)/shard_map/reduce_scatter | solution.py:13
  183.6 0.7 copy-start.5
  183.6 52.6 %copy-start.2 = (bf16[16,2048]{1,0:T(8,128)(2,1)S(1)}, bf16[16,2048]{1,0:T(8,128)(2,1)}, u32[]{:S(2)}) copy-start(bf16[16,2048]{1,0:T(8,128)(2,1)} %param.12) | copy-start | bytes 196612
  183.6 56.8 %copy-start.4 = (bf16[512,2752]{0,1:T(8,128)(2,1)S(1)}, bf16[512,2752]{0,1:T(8,128)(2,1)}, u32[]{:S(2)}) copy-start(bf16[512,2752]{0,1:T(8,128)(2,1)} %all-gather.5.cloned.1.call-done) | copy-start | bytes 8454148
Sparse Core Ops, SparseCore 0:
  9.5 13.7 all-gather.4
  27.2 63.2 reduce-scatter.5
  92.6 71.8 all-gather.2
  168.4 67.8 all-reduce.2
  238.4 13.1 reduce-scatter.3
where the time goes:
time: 268 us
  waiting for transfers between devices  198 us (74%)
  matrix products  42.3 us (16%)
  between operations  14.5 us (5%)
  blocking collectives  5.99 us (2%)
  other arithmetic  3.36 us (1%)
  local copies, waits for them, and re-layouts  3.16 us (1%)
    all_gather x1, waiting for transfers between devices, body(): full_grad = lax.all_gather(grad_out, 'row', axis=0, tiled=True)  71.5 us
    reduce_scatter x1, waiting for transfers between devices, body(): lax.psum_scatter(jnp.dot(token_rows, proj_in, preferred_element_type=jnp....  59.1 us
    psum x1, waiting for transfers between devices, body(): example_grads = lax.psum(partial_grads, 'row')  50.7 us
    dot_general x1, matrix products, body(): lax.dot_general(token_rows, down_weight, (((1,), (1,)), ((), ())), prefer...  19.1 us
    dot_general x1, matrix products, body(): lax.dot_general(full_hidden, full_grad, (((0,), (0,)), ((), ())), preferr...  17.6 us
    all_gather x1, waiting for transfers between devices, body(): full_hidden = lax.all_gather(hidden_act, 'col', axis=0, tiled=True)  15.3 us
  transfers between devices with their start and end apart: 5, of which 4 were waited for; matrix products, arithmetic and copies ran while one was open for 16% of the time, Pallas kernels for 0%

commit v1 on v0

--- a/solution.py
+++ b/solution.py
@@ -8,7 +8,13 @@
 
 def body(grad_out, hidden_act, down_weight, proj_in, proj_out, queries, example_ids):
     full_hidden = lax.all_gather(hidden_act, "col", axis=0, tiled=True)
-    full_grad = lax.all_gather(grad_out, "row", axis=0, tiled=True)
+    count = lax.axis_size("row")
+    moving, parts = (grad_out, [grad_out])
+    for _ in range(count - 1):
+        moving = lax.ppermute(moving, "row", [(i, (i + 1) % count) for i in range(count)])
+        parts.insert(0, moving)
+    row_of_blocks = jnp.concatenate(parts, axis=0)
+    full_grad = jnp.roll(row_of_blocks, (lax.axis_index("row") + 1) * grad_out.shape[0], axis=0)
     token_rows = full_grad
     grad_hidden = lax.psum_scatter(
         lax.dot_general(

time: 268 us -> 258 us (0.963)
  waiting for transfers between devices: 198 us -> 171 us
  local copies, waits for them, and re-layouts: 3.16 us -> 14.5 us
  starting transfers between devices: 0.2 us -> 3.19 us
    ppermute x0 -> x7, waiting for transfers between devices: none -> 77.1 us  [body(): lax.ppermute(moving, 'row', [(i, (i + 1) % count) for i in range(count)])]
    all_gather x1 -> x0, waiting for transfers between devices: 71.5 us -> none  [body(): full_grad = lax.all_gather(grad_out, 'row', axis=0, tiled=True)]
    all_gather x1, waiting for transfers between devices: 15.3 us -> 0.01 us  [body(): full_hidden = lax.all_gather(hidden_act, 'col', axis=0, tiled=True)]
    psum x1, waiting for transfers between devices: 50.7 us -> 38.7 us  [body(): example_grads = lax.psum(partial_grads, 'row')]
    unnamed x15 -> x44, local copies, waits for them, and re-layouts: 1.97 us -> 13.3 us
    reduce_scatter x1, waiting for transfers between devices: 59.1 us -> 55 us  [body(): lax.psum_scatter(jnp.dot(token_rows, proj_in, preferred_element_type=jnp....]
    ppermute x0 -> x7, starting transfers between devices: none -> 3.04 us  [body(): lax.ppermute(moving, 'row', [(i, (i + 1) % count) for i in range(count)])]
  transfers between devices with their start and end apart: 5 -> 11, of which waited for: 4 -> 8; matrix products, arithmetic and copies ran while one was open for 16% -> 21% of each run, Pallas kernels for 0% -> 0%
where the time goes in v1:
time: 258 us; the launch traced here: 257 us
  waiting for transfers between devices  171 us (66%)
  matrix products  43.8 us (17%)
  between operations  14.7 us (6%)
  local copies, waits for them, and re-layouts  14.5 us (6%)
  blocking collectives  5.91 us (2%)
  other arithmetic  3.36 us (1%)
  starting transfers between devices  3.19 us (1%)
    ppermute x7, waiting for transfers between devices, body(): lax.ppermute(moving, 'row', [(i, (i + 1) % count) for i in range(count)])  77.1 us
    reduce_scatter x1, waiting for transfers between devices, body(): lax.psum_scatter(jnp.dot(token_rows, proj_in, preferred_element_type=jnp....  55 us
    psum x1, waiting for transfers between devices, body(): example_grads = lax.psum(partial_grads, 'row')  38.7 us
    dot_general x1, matrix products, body(): lax.dot_general(full_hidden, full_grad, (((0,), (0,)), ((), ())), preferr...  18.9 us
    dot_general x1, matrix products, body(): lax.dot_general(token_rows, down_weight, (((1,), (1,)), ((), ())), prefer...  18 us
    unnamed x44, local copies, waits for them, and re-layouts  13.3 us
  transfers between devices with their start and end apart: 11, of which 8 were waited for; matrix products, arithmetic and copies ran while one was open for 21% of the time, Pallas kernels for 0%

profile of v1, /device:TPU:0, one launch (start us, length us, event | category | flops | bytes accessed | tf_op | source)
XLA Modules:
  0.0 256.9 jit_solution(655318566692774925)
XLA Ops:
  7.2 0.0 copy-start
  7.2 0.0 copy-start.2
  7.2 0.0 copy-start.11
  7.2 0.0 all-gather.2.cloned.1.call-start
  7.2 0.7 all-gather.2.cloned.1.call-update
  7.9 0.0 reduce-scatter.6.cloned.1.call-start
  8.0 3.0 %collective-permute-start = (bf16[64,4096]{1,0:T(8,128)(2,1)}, bf16[64,4096]{1,0:T(8,128)(2,1)S(1)}, u32[]{:S(2)}, u32[]{:S(2)}) collective-permute-start(bf16[64,4096]{1,0:T(8,128)(2,1)} %param.7), channel_id=1, source_target_pairs={{0,2},{2,4},{4,6},{6,8},{8,10},{10,12},{12,14},{14,0},{1,3},{3,5},... | collective-permute-start | bytes 1572872 | tf_op jit(solution)/shard_map/ppermute | solution.py:14
  11.0 15.2 %collective-permute-done = bf16[64,4096]{1,0:T(8,128)(2,1)S(1)} collective-permute-done((bf16[64,4096]{1,0:T(8,128)(2,1)}, bf16[64,4096]{1,0:T(8,128)(2,1)S(1)}, u32[]{:S(2)}, u32[]{:S(2)}) %collective-permute-start) | collective-permute-done | bytes 524320 | tf_op jit(solution)/shard_map/ppermute | solution.py:14
  26.2 0.0 collective-permute-start.1
  26.2 15.8 %collective-permute-done.1 = bf16[64,4096]{1,0:T(8,128)(2,1)S(1)} collective-permute-done((bf16[64,4096]{1,0:T(8,128)(2,1)S(1)}, bf16[64,4096]{1,0:T(8,128)(2,1)S(1)}, u32[]{:S(2)}, u32[]{:S(2)}) %collective-permute-start.1) | collective-permute-done | bytes 524320 | tf_op jit(solution)/shard_map/ppermute | solution.py:14
  42.0 0.0 collective-permute-start.2
  42.0 14.9 %collective-permute-done.2 = bf16[64,4096]{1,0:T(8,128)(2,1)S(1)} collective-permute-done((bf16[64,4096]{1,0:T(8,128)(2,1)S(1)}, bf16[64,4096]{1,0:T(8,128)(2,1)S(1)}, u32[]{:S(2)}, u32[]{:S(2)}) %collective-permute-start.2) | collective-permute-done | bytes 524320 | tf_op jit(solution)/shard_map/ppermute | solution.py:14
  56.9 0.8 copy-done.3
  57.7 0.0 collective-permute-start.3
  57.7 14.1 %collective-permute-done.3 = bf16[64,4096]{1,0:T(8,128)(2,1)S(1)} collective-permute-done((bf16[64,4096]{1,0:T(8,128)(2,1)S(1)}, bf16[64,4096]{1,0:T(8,128)(2,1)S(1)}, u32[]{:S(2)}, u32[]{:S(2)}) %collective-permute-start.3) | collective-permute-done | bytes 524320 | tf_op jit(solution)/shard_map/ppermute | solution.py:14
  71.8 0.0 collective-permute-start.4
  71.8 13.2 %collective-permute-done.4 = bf16[64,4096]{1,0:T(8,128)(2,1)S(1)} collective-permute-done((bf16[64,4096]{1,0:T(8,128)(2,1)S(1)}, bf16[64,4096]{1,0:T(8,128)(2,1)S(1)}, u32[]{:S(2)}, u32[]{:S(2)}) %collective-permute-start.4) | collective-permute-done | bytes 524320 | tf_op jit(solution)/shard_map/ppermute | solution.py:14
  85.0 0.0 collective-permute-start.5
  85.0 3.7 %fusion.8 = f32[512,64]{1,0:T(8,128)} fusion(bf16[512,2752]{0,1:T(8,128)(2,1)} %all-gather.2.cloned.1.call-done, bf16[2752,64]{0,1:T(8,128)(2,1)} %param.10), kind=kOutput, calls=%fused_computation.30 | convolution fusion | flops 180355072 | bytes 3301376 | tf_op jit(solution)/shard_map/dot_general | solution.py:32
  88.7 0.0 reduce-scatter.6.cloned.1.call-update
  88.7 0.0 all-reduce.3.cloned.1.call-start
  88.7 0.0 copy-done
  88.7 1.3 fusion.9
  90.1 3.4 %psum.14 = f32[64,64]{1,0:T(8,128)S(1)} all-reduce(f32[64,64]{1,0:T(8,128)S(1)} %fusion.9), channel_id=1, replica_groups=mesh['grp'=2,'row'=8,'col'=2] {'col'}, use_global_device_ids=true, to_apply=%region_2.3 | all-reduce | flops 4096 | bytes 32768 | tf_op jit(solution)/shard_map/psum | solution.py:37
  93.5 4.0 %collective-permute-done.5 = bf16[64,4096]{1,0:T(8,128)(2,1)} collective-permute-done((bf16[64,4096]{1,0:T(8,128)(2,1)S(1)}, bf16[64,4096]{1,0:T(8,128)(2,1)}, u32[]{:S(2)}, u32[]{:S(2)}) %collective-permute-start.5) | collective-permute-done | bytes 524320 | tf_op jit(solution)/shard_map/ppermute | solution.py:14
  97.4 0.0 collective-permute-start.6
  97.5 55.0 %reduce-scatter.6.cloned.1.call-done = f32[64,64]{1,0:T(8,128)} async-done(((f32[512,64]{1,0:T(8,128)}), f32[64,64]{1,0:T(8,128)}) %reduce-scatter.6.cloned.1.call-update) | async-done | bytes 16400 | tf_op jit(solution)/shard_map/reduce_scatter | solution.py:31
  152.4 0.0 copy-done.5
  152.4 0.0 copy-done.7
  152.4 0.8 constant_dynamic-slice_fusion.1
  153.3 0.3 broadcast_multiply_fusion
  153.6 0.4 mul.28
  154.0 0.0 copy-done.11
  154.0 0.0 copy-start.6
  154.0 0.0 copy-start.4
  154.0 0.9 fusion.4
  154.9 0.0 all-reduce.3.cloned.1.call-update
  154.9 0.0 reduce-scatter.4.cloned.1.call-start
  155.0 0.0 collective-permute-done.6
  155.0 1.1 constant_dynamic-update-slice_fusion.15
  156.1 1.1 constant_dynamic-update-slice_fusion.14
  157.2 1.1 constant_dynamic-update-slice_fusion.13
  158.3 1.1 constant_dynamic-update-slice_fusion.12
  159.4 1.1 constant_dynamic-update-slice_fusion.11
  160.5 0.0 copy-done.2
  160.6 1.1 constant_dynamic-update-slice_fusion.7
  161.7 1.1 constant_dynamic-update-slice_fusion.6
  162.8 0.0 copy-done.8
  162.8 0.0 copy-done.6
  162.9 0.0 copy-done.4
  163.0 0.0 copy-start.10
  163.1 3.2 %copy-done.10 = bf16[1024,4096]{1,0:T(8,128)(2,1)} copy-done((bf16[1024,4096]{1,0:T(8,128)(2,1)}, bf16[1024,4096]{1,0:T(8,128)(2,1)S(1)}, u32[]{:S(2)}) %copy-start.10) | copy-done | bytes 8388632
  166.3 18.0 %fusion.2 = f32[512,2752]{0,1:T(8,128)} fusion(bf16[2752,4096]{1,0:T(8,128)(2,1)} %param.9, bf16[1024,4096]{1,0:T(8,128)(2,1)S(1)} %constant_dynamic-update-slice_fusion, s32[]{:T(128)S(6)} %select_n.17), kind=kOutput, calls=%fused_computation.3 | convolution fusion | flops 11542724608 | bytes 32374788 | tf_op jit(solution)/shard_map/dot_general | solution.py:20
  184.3 0.0 reduce-scatter.4.cloned.1.call-update
  184.3 0.0 copy-done.12
  184.3 0.6 dynamic-slice
  185.6 38.7 %all-reduce.3.cloned.1.call-done = f32[8,2048]{1,0:T(8,128)} async-done(((f32[8,2048]{1,0:T(8,128)}), f32[8,2048]{1,0:T(8,128)}) %all-reduce.3.cloned.1.call-update) | async-done | bytes 65552 | tf_op jit(solution)/shard_map/psum | solution.py:46
  224.2 0.0 copy-done.9
  224.2 1.0 convolution_bitcast_fusion
  225.2 2.5 all-reduce
  227.7 0.1 constant_dynamic-slice_fusion
  227.7 0.7 copy.11
  228.4 18.9 %fusion = bf16[2752,4096]{1,0:T(8,128)(2,1)} fusion(bf16[512,2752]{0,1:T(8,128)(2,1)} %all-gather.2.cloned.1.call-done, bf16[1024,4096]{1,0:T(8,128)(2,1)} %copy-done.10, s32[]{:T(128)S(6)} %select_n.17), kind=kOutput, calls=%fused_computation.1 | convolution fusion | flops 11553996800 | bytes 29556740 | tf_op jit(solution)/shard_map/dot_general | solution.py:27
  247.3 3.0 %convert_element_type.11 = bf16[256,2752]{0,1:T(8,128)(2,1)} convert(f32[256,2752]{0,1:T(8,128)} %reduce-scatter.4.cloned.1.call-done) | non-fusion elementwise | flops 704512 | bytes 4227072 | tf_op jit(solution)/shard_map/convert_element_type | solution.py:26
  (19 shorter events, 0.3 us)
Async XLA Ops:
  7.2 81.6 %copy-start = (bf16[4096,64]{0,1:T(8,128)(2,1)S(1)}, bf16[4096,64]{0,1:T(8,128)(2,1)}, u32[]{:S(2)}) copy-start(bf16[4096,64]{0,1:T(8,128)(2,1)} %param.11) | copy-start | bytes 1572868
  7.2 153.4 %copy-start.2 = (bf16[64,4096]{1,0:T(8,128)(2,1)S(1)}, bf16[64,4096]{1,0:T(8,128)(2,1)}, u32[]{:S(2)}) copy-start(bf16[64,4096]{1,0:T(8,128)(2,1)} %param.7) | copy-start | bytes 1572868
  7.2 146.8 %copy-start.11 = (s32[64]{0:T(128)S(1)}, s32[64]{0:T(128)}, u32[]{:S(2)}) copy-start(s32[64]{0:T(128)} %param.13) | copy-start | bytes 772
  7.2 77.8 %all-gather.2.cloned.1.call-start = ((), (), s32[]{:S(2)}) async-start(), calls=%async_computation.3 | async-start | bytes 4227072 | tf_op jit(solution)/shard_map/all_gather | solution.py:10
  7.9 144.5 %reduce-scatter.6.cloned.1.call-start = ((), (), s32[]{:S(2)}) async-start(), calls=%async_computation.4 | async-start | bytes 294912 | tf_op jit(solution)/shard_map/reduce_scatter | solution.py:31
  8.0 18.2 %collective-permute-start = (bf16[64,4096]{1,0:T(8,128)(2,1)}, bf16[64,4096]{1,0:T(8,128)(2,1)S(1)}, u32[]{:S(2)}, u32[]{:S(2)}) collective-permute-start(bf16[64,4096]{1,0:T(8,128)(2,1)} %param.7), channel_id=1, source_target_pairs={{0,2},{2,4},{4,6},{6,8},{8,10},{10,12},{12,14},{14,0},{1,3},{3,5},... | collective-permute-start | bytes 1572872 | tf_op jit(solution)/shard_map/ppermute | solution.py:14
  26.2 15.8 %collective-permute-start.1 = (bf16[64,4096]{1,0:T(8,128)(2,1)S(1)}, bf16[64,4096]{1,0:T(8,128)(2,1)S(1)}, u32[]{:S(2)}, u32[]{:S(2)}) collective-permute-start(bf16[64,4096]{1,0:T(8,128)(2,1)S(1)} %collective-permute-done), channel_id=1, source_target_pairs={{0,2},{2,4},{4,6},{6,8},{8,10},{10,12},{12,14},{14,0},{1,3},{3,5},... | collective-permute-start | bytes 1572872 | tf_op jit(solution)/shard_map/ppermute | solution.py:14
  42.0 14.9 %collective-permute-start.2 = (bf16[64,4096]{1,0:T(8,128)(2,1)S(1)}, bf16[64,4096]{1,0:T(8,128)(2,1)S(1)}, u32[]{:S(2)}, u32[]{:S(2)}) collective-permute-start(bf16[64,4096]{1,0:T(8,128)(2,1)S(1)} %collective-permute-done.1), channel_id=1, source_target_pairs={{0,2},{2,4},{4,6},{6,8},{8,10},{10,12},{12,14},{14,0},{1,3},{3,5},... | collective-permute-start | bytes 1572872 | tf_op jit(solution)/shard_map/ppermute | solution.py:14
  56.9 0.8 copy-start.3
  57.7 14.1 %collective-permute-start.3 = (bf16[64,4096]{1,0:T(8,128)(2,1)S(1)}, bf16[64,4096]{1,0:T(8,128)(2,1)S(1)}, u32[]{:S(2)}, u32[]{:S(2)}) collective-permute-start(bf16[64,4096]{1,0:T(8,128)(2,1)S(1)} %collective-permute-done.2), channel_id=1, source_target_pairs={{0,2},{2,4},{4,6},{6,8},{8,10},{10,12},{12,14},{14,0},{1,3},{3,5},... | collective-permute-start | bytes 1572872 | tf_op jit(solution)/shard_map/ppermute | solution.py:14
  71.8 80.7 %copy-start.5 = (bf16[64,4096]{1,0:T(8,128)(2,1)}, bf16[64,4096]{1,0:T(8,128)(2,1)S(1)}, u32[]{:S(2)}) copy-start(bf16[64,4096]{1,0:T(8,128)(2,1)S(1)} %collective-permute-done.3) | copy-start | bytes 1572868
  71.8 13.2 %collective-permute-start.4 = (bf16[64,4096]{1,0:T(8,128)(2,1)S(1)}, bf16[64,4096]{1,0:T(8,128)(2,1)S(1)}, u32[]{:S(2)}, u32[]{:S(2)}) collective-permute-start(bf16[64,4096]{1,0:T(8,128)(2,1)S(1)} %collective-permute-done.3), channel_id=1, source_target_pairs={{0,2},{2,4},{4,6},{6,8},{8,10},{10,12},{12,14},{14,0},{1,3},{3,5},... | collective-permute-start | bytes 1572872 | tf_op jit(solution)/shard_map/ppermute | solution.py:14
  85.0 67.4 %copy-start.7 = (bf16[64,4096]{1,0:T(8,128)(2,1)}, bf16[64,4096]{1,0:T(8,128)(2,1)S(1)}, u32[]{:S(2)}) copy-start(bf16[64,4096]{1,0:T(8,128)(2,1)S(1)} %collective-permute-done.4) | copy-start | bytes 1572868
  85.0 12.5 %collective-permute-start.5 = (bf16[64,4096]{1,0:T(8,128)(2,1)S(1)}, bf16[64,4096]{1,0:T(8,128)(2,1)}, u32[]{:S(2)}, u32[]{:S(2)}) collective-permute-start(bf16[64,4096]{1,0:T(8,128)(2,1)S(1)} %collective-permute-done.4), channel_id=1, source_target_pairs={{0,2},{2,4},{4,6},{6,8},{8,10},{10,12},{12,14},{14,0},{1,3},{3,5},... | collective-permute-start | bytes 1572872 | tf_op jit(solution)/shard_map/ppermute | solution.py:14
  88.7 135.5 %all-reduce.3.cloned.1.call-start = ((), (), s32[]{:S(2)}) async-start(), calls=%async_computation.5 | async-start | bytes 131072 | tf_op jit(solution)/shard_map/psum | solution.py:46
  97.4 57.5 %collective-permute-start.6 = (bf16[64,4096]{1,0:T(8,128)(2,1)}, bf16[64,4096]{1,0:T(8,128)(2,1)}, u32[]{:S(2)}, u32[]{:S(2)}) collective-permute-start(bf16[64,4096]{1,0:T(8,128)(2,1)} %collective-permute-done.5), channel_id=1, source_target_pairs={{0,2},{2,4},{4,6},{6,8},{8,10},{10,12},{12,14},{14,0},{1,3},{3,5},... | collective-permute-start | bytes 1572872 | tf_op jit(solution)/shard_map/ppermute | solution.py:14
  154.0 8.8 %copy-start.6 = (bf16[64,4096]{1,0:T(8,128)(2,1)S(1)}, bf16[64,4096]{1,0:T(8,128)(2,1)}, u32[]{:S(2)}) copy-start(bf16[64,4096]{1,0:T(8,128)(2,1)} %copy-done.5) | copy-start | bytes 1572868
  154.0 8.9 %copy-start.4 = (bf16[64,4096]{1,0:T(8,128)(2,1)S(1)}, bf16[64,4096]{1,0:T(8,128)(2,1)}, u32[]{:S(2)}) copy-start(bf16[64,4096]{1,0:T(8,128)(2,1)} %copy-done.3) | copy-start | bytes 1572868
  154.9 7.8 %copy-start.8 = (bf16[64,4096]{1,0:T(8,128)(2,1)S(1)}, bf16[64,4096]{1,0:T(8,128)(2,1)}, u32[]{:S(2)}) copy-start(bf16[64,4096]{1,0:T(8,128)(2,1)} %copy-done.7) | copy-start | bytes 1572868
  154.9 92.4 %reduce-scatter.4.cloned.1.call-start = ((), (), s32[]{:S(2)}) async-start(), calls=%async_computation.2 | async-start | bytes 8454144 | tf_op jit(solution)/shard_map/reduce_scatter | solution.py:19
  163.0 3.2 %copy-start.10 = (bf16[1024,4096]{1,0:T(8,128)(2,1)}, bf16[1024,4096]{1,0:T(8,128)(2,1)S(1)}, u32[]{:S(2)}) copy-start(bf16[1024,4096]{1,0:T(8,128)(2,1)S(1)} %constant_dynamic-update-slice_fusion) | copy-start | bytes 25165828
  166.3 18.0 %copy-start.12 = (u32[32]{0:T(128)S(1)}, u32[32]{0:T(128)}, u32[]{:S(2)}) copy-start(u32[32]{0:T(128)} %constant.39) | copy-start | bytes 388
  166.3 57.9 %copy-start.9 = (bf16[16,2048]{1,0:T(8,128)(2,1)S(1)}, bf16[16,2048]{1,0:T(8,128)(2,1)}, u32[]{:S(2)}) copy-start(bf16[16,2048]{1,0:T(8,128)(2,1)} %param.12) | copy-start | bytes 196612
  228.4 21.9 %copy-start.1 = (bf16[4096,64]{0,1:T(8,128)(2,1)S(1)}, bf16[4096,64]{0,1:T(8,128)(2,1)}, u32[]{:S(2)}) copy-start(bf16[4096,64]{0,1:T(8,128)(2,1)} %param.11) | copy-start | bytes 1572868
Sparse Core Ops, SparseCore 0:
  9.5 13.7 all-gather.1
  88.8 63.5 reduce-scatter.5
  155.8 68.3 all-reduce.2
  226.4 13.1 reduce-scatter.3
